TPU v7x, 32 devices: a whole 2x2x4 slice. The times are simulated.
32 devices in a mesh: dp: 8 (over z, y), tp: 4 (over x, core).
Axes of the slice: x: 2, y: 2, z: 4, core: 2. Of those that a mesh axis runs over, the one named last changes fastest.
Arguments:
- frames: bfloat16 [16, 2304, 384], P('dp', 'tp'), may hold values from -6 to 6
- targets: bfloat16 [16, 2304, 384], P('dp', 'tp'), may hold values from -6 to 6
- presence: int32 [16, 4], P('dp'), may hold values 0 or 1
- order: int32 [8, 2], P('dp'), may hold values from 0 to 1, each once within a row
- attn_proj: float32 [3, 384, 384], P(None, None, 'tp'), may hold values from -0.3125 to 0.3125
- out_proj: float32 [384, 384], P('tp'), may hold values from -7 to 7
- up_proj: float32 [384, 1536], P(None, 'tp'), may hold values from -0.3125 to 0.3125
- up_bias: float32 [1536], P('tp'), may hold values from -3 to 3
- down_proj: float32 [384, 1536], P(None, 'tp'), may hold values from -0.15625 to 0.15625
- head_proj: float32 [384, 384], replicated, may hold values from -0.3125 to 0.3125
- vectors: float32 [9, 384], replicated
- momentum_attn: float32 [3, 384, 384], P(None, None, 'tp'), may hold values from -256 to 256
- momentum_out: float32 [384, 384], P('tp'), may hold values from -3 to 3
- momentum_up: float32 [384, 1536], P(None, 'tp'), may hold values from -3 to 3
- momentum_bias: float32 [1536], P('tp'), may hold values from -3 to 3
- momentum_down: float32 [384, 1536], P(None, 'tp'), may hold values from -3 to 3
- momentum_head: float32 [384, 384], replicated, may hold values from -224 to 224
- momentum_vectors: float32 [9, 384], replicated, may hold values from -3 to 3
- average_attn: float32 [3, 384, 384], P(None, None, 'tp'), may hold values from -0.3125 to 0.3125
- average_out: float32 [384, 384], P('tp'), may hold values from -7 to 7
- average_up: float32 [384, 1536], P(None, 'tp'), may hold values from -0.3125 to 0.3125
- average_bias: float32 [1536], P('tp'), may hold values from -3 to 3
- average_down: float32 [384, 1536], P(None, 'tp'), may hold values from -0.15625 to 0.15625
- average_head: float32 [384, 384], replicated, may hold values from -0.3125 to 0.3125
- average_vectors: float32 [9, 384], replicated
Outputs:
- loss: float32 [], replicated
- new_attn: float32 [3, 384, 384], P(None, None, 'tp')
- new_out: float32 [384, 384], P('tp')
- new_up: float32 [384, 1536], P(None, 'tp')
- new_bias: float32 [1536], P('tp')
- new_down: float32 [384, 1536], P(None, 'tp')
- new_head: float32 [384, 384], replicated
- new_vectors: float32 [9, 384], replicated
- moment_attn: float32 [3, 384, 384], P(None, None, 'tp')
- moment_out: float32 [384, 384], P('tp')
- moment_up: float32 [384, 1536], P(None, 'tp')
- moment_bias: float32 [1536], P('tp')
- moment_down: float32 [384, 1536], P(None, 'tp')
- moment_head: float32 [384, 384], replicated
- moment_vectors: float32 [9, 384], replicated
- mean_attn: float32 [3, 384, 384], P(None, None, 'tp')
- mean_out: float32 [384, 384], P('tp')
- mean_up: float32 [384, 1536], P(None, 'tp')
- mean_bias: float32 [1536], P('tp')
- mean_down: float32 [384, 1536], P(None, 'tp')
- mean_head: float32 [384, 384], replicated
- mean_vectors: float32 [9, 384], replicated
- grad_frames: float32 [16, 2304, 384], P('dp', 'tp')
Inputs may be any that keep to these rules, and one draw needn't show every extreme that they name: `order`: each row holds every number below 2 once.
All inputs are finite; a program needn't handle non-finite values. No bound on the sum of `presence` on one device may be relied on, other than what follows from the above.
Results may differ from a plain program's by a relative error of at most 0.0095.
Values may be sent and summed in bfloat16 or wider, within the bound.
No kernel may reach another device: no remote copies, remote signals or barrier semaphores. Data moves between devices by JAX's collectives and lax.ppermute only.
A program may use at most 192 MiB of HBM per device.

v0:
```python
import jax
import jax.numpy as jnp
from jax import lax
from jax.sharding import PartitionSpec as P

CHN = 96
HDIM = 48
HEAD = 384
EPSILON = 1e-05
MOMENTUM_RATE = 0.9
LEARN_RATE = 0.02
AVERAGE_RATE = 0.9


def product(left, right, form):
    return jnp.einsum(form, left, right, preferred_element_type=jnp.float32)


def norm_forward(values, gain, shift):
    centred = values - jnp.mean(values, axis=-1, keepdims=True)
    inverse = lax.rsqrt(jnp.mean(centred * centred, axis=-1, keepdims=True) + EPSILON)
    normed = centred * inverse
    return (normed * gain + shift, normed, inverse)


def norm_backward(grad, normed, inverse, gain):
    scaled = grad * gain
    back = inverse * (
        scaled
        - jnp.mean(scaled, axis=-1, keepdims=True)
        - normed * jnp.mean(scaled * normed, axis=-1, keepdims=True)
    )
    return (back, jnp.sum(grad * normed, axis=(0, 1)), jnp.sum(grad, axis=(0, 1)))


def head_forward(packed):
    query_rows, key_rows, value_rows = packed
    scores = product(query_rows, key_rows, "qd,kd->qk") * HDIM ** (-0.5)
    maximum = jnp.max(scores, axis=-1, keepdims=True)
    exponent = jnp.exp(scores - maximum)
    totals = jnp.sum(exponent, axis=-1, keepdims=True)
    weights = (exponent / totals).astype(jnp.bfloat16)
    mixed = product(weights, value_rows, "qk,kd->qd").astype(jnp.bfloat16)
    return (mixed, (maximum + jnp.log(totals))[:, 0])


def head_backward(packed):
    query_rows, key_rows, value_rows, logsum, grad_out = packed
    factor = HDIM ** (-0.5)
    probs = jnp.exp(product(query_rows, key_rows, "qd,kd->qk") * factor - logsum[:, None])
    grad_value = product(probs.astype(jnp.bfloat16), grad_out, "qk,qd->kd")
    grad_probs = product(grad_out, value_rows, "qd,kd->qk")
    grad_scores = (
        probs * (grad_probs - jnp.sum(probs * grad_probs, axis=-1, keepdims=True))
    ).astype(jnp.bfloat16)
    grad_query = product(grad_scores, key_rows, "qk,kd->qd") * factor
    grad_key = product(grad_scores, query_rows, "qk,qd->kd") * factor
    return jnp.stack([grad_query, grad_key, grad_value]).astype(jnp.bfloat16)


def to_heads(packed, items, heads_here):
    length = packed.shape[2]
    split = packed.reshape(3, items, length, heads_here, HDIM).transpose(0, 1, 3, 2, 4)
    return split.reshape(3, items * heads_here, length, HDIM)


def from_heads(stacked, items, heads_here):
    length = stacked.shape[-2]
    split = stacked.reshape(stacked.shape[:-3] + (items, heads_here, length, HDIM))
    moved = jnp.moveaxis(split, -2, -3)
    return moved.reshape(stacked.shape[:-3] + (items, length, heads_here * HDIM))


def update(weight, moment, average, grad):
    moment_new = MOMENTUM_RATE * moment + grad
    weight_new = weight - LEARN_RATE * (grad + MOMENTUM_RATE * moment_new)
    average_new = AVERAGE_RATE * average + (1.0 - AVERAGE_RATE) * weight_new
    return (weight_new, moment_new, average_new)


def per_device(
    frames,
    targets,
    presence,
    order,
    attn_proj,
    out_proj,
    up_proj,
    up_bias,
    down_proj,
    head_proj,
    vectors,
    momentum_attn,
    momentum_out,
    momentum_up,
    momentum_bias,
    momentum_down,
    momentum_head,
    momentum_vectors,
    average_attn,
    average_out,
    average_up,
    average_bias,
    average_down,
    average_head,
    average_vectors,
):
    items = frames.shape[0]
    heads_here = out_proj.shape[0] // HDIM
    bf16 = jnp.bfloat16
    start = frames.astype(jnp.float32)
    goal = jnp.take(targets, order[0], axis=0).astype(jnp.float32)
    keep = (presence.astype(jnp.float32)[:, :, None] * jnp.ones((1, 1, CHN), jnp.float32)).reshape(
        items, 1, HEAD
    )
    head_low = head_proj.astype(bf16)
    attn_low = attn_proj.astype(bf16)
    out_low = out_proj.astype(bf16)
    first, hat_one, inv_one = norm_forward(start, vectors[0], vectors[1])
    first_low = first.astype(bf16)
    first_all = lax.all_gather(first_low, "tp", axis=1, tiled=True)
    packed = product(first_all, attn_low, "bsd,jde->jbse").astype(bf16)
    heads = to_heads(packed, items, heads_here)
    mixed, logsum = lax.map(head_forward, (heads[0], heads[1], heads[2]))
    attended = from_heads(mixed, items, heads_here)
    attn_term = lax.psum_scatter(
        product(attended, out_low, "bse,ed->bsd"), "tp", scatter_dimension=1, tiled=True
    )
    middle = start + vectors[3] * (attn_term + vectors[2])
    second, hat_two, inv_two = norm_forward(middle, vectors[4], vectors[5])
    second_low = second.astype(bf16)
    up_all = up_proj.astype(bf16)
    down_all = down_proj.astype(bf16)
    second_all = lax.all_gather(second_low, "tp", axis=1, tiled=True)
    hidden_pre = product(second_all, up_all, "bsd,df->bsf") + up_bias
    hidden = jax.nn.gelu(hidden_pre).astype(bf16)
    ffn_term = lax.psum_scatter(
        product(hidden, down_all, "bsf,df->bsd"), "tp", scatter_dimension=1, tiled=True
    )
    final = middle + vectors[7] * (ffn_term + vectors[6])
    final_low = final.astype(bf16)
    pred = product(final_low, head_low, "bsd,dh->bsh") + vectors[8]
    diff = pred - goal
    smooth = jnp.sqrt(diff * diff + 1.0)
    part_loss = jnp.sum(keep * (smooth - 1.0)) / HEAD
    grad_pred = (keep * (diff / smooth) / HEAD).astype(bf16)
    grad_head = product(final_low, grad_pred, "bsd,bsh->dh")
    grad_head_bias = jnp.sum(grad_pred.astype(jnp.float32), axis=(0, 1))
    grad_final = product(grad_pred, head_low, "bsh,dh->bsd")
    grad_scale_two = jnp.sum(grad_final * (ffn_term + vectors[6]), axis=(0, 1))
    grad_ffn = grad_final * vectors[7]
    grad_down_bias = jnp.sum(grad_ffn, axis=(0, 1))
    ffn_low = grad_ffn.astype(bf16)
    gelu_pull = jax.vjp(jax.nn.gelu, hidden_pre)[1]
    ffn_all = lax.all_gather(ffn_low, "tp", axis=1, tiled=True)
    grad_hidden = product(ffn_all, down_all, "bsd,df->bsf")
    grad_down = product(ffn_all, hidden, "bsd,bsf->df")
    grad_pre = gelu_pull(grad_hidden)[0].astype(bf16)
    grad_up = product(second_all, grad_pre, "bsd,bsf->df")
    grad_up_bias = jnp.sum(grad_pre.astype(jnp.float32), axis=(0, 1))
    grad_second = lax.psum_scatter(
        product(grad_pre, up_all, "bsf,df->bsd"), "tp", scatter_dimension=1, tiled=True
    )
    back_two, grad_gain_two, grad_shift_two = norm_backward(
        grad_second, hat_two, inv_two, vectors[4]
    )
    grad_middle = grad_final + back_two
    grad_scale_one = jnp.sum(grad_middle * (attn_term + vectors[2]), axis=(0, 1))
    grad_attn = grad_middle * vectors[3]
    grad_out_bias = jnp.sum(grad_attn, axis=(0, 1))
    attn_grad_low = grad_attn.astype(bf16)
    attn_all = lax.all_gather(attn_grad_low, "tp", axis=1, tiled=True)
    grad_out = product(attended, attn_all, "bse,bsd->ed")
    grad_attended = product(attn_all, out_low, "bsd,ed->bse").astype(bf16)
    grad_mixed = to_heads(jnp.stack([grad_attended] * 3), items, heads_here)[0]
    grad_heads = lax.map(head_backward, (heads[0], heads[1], heads[2], logsum, grad_mixed))
    grad_packed = from_heads(jnp.moveaxis(grad_heads, 1, 0), items, heads_here)
    grad_attn_proj = product(first_all, grad_packed, "bsd,jbse->jde")
    grad_first = lax.psum_scatter(
        product(grad_packed, attn_low, "jbse,jde->bsd").astype(jnp.bfloat16),
        "tp",
        scatter_dimension=1,
        tiled=True,
    ).astype(jnp.float32)
    back_one, grad_gain_one, grad_shift_one = norm_backward(
        grad_first, hat_one, inv_one, vectors[0]
    )
    grad_frames = grad_middle + back_one
    grad_vectors = jnp.stack(
        [
            grad_gain_one,
            grad_shift_one,
            grad_out_bias,
            grad_scale_one,
            grad_gain_two,
            grad_shift_two,
            grad_down_bias,
            grad_scale_two,
            grad_head_bias,
        ]
    )
    grad_attn_proj, grad_out, grad_up, grad_up_bias, grad_down = lax.psum(
        (grad_attn_proj, grad_out, grad_up, grad_up_bias, grad_down), "dp"
    )
    grad_head, grad_vectors, loss = lax.psum((grad_head, grad_vectors, part_loss), ("dp", "tp"))
    first_set = update(attn_proj, momentum_attn, average_attn, grad_attn_proj)
    second_set = update(out_proj, momentum_out, average_out, grad_out)
    third_set = update(up_proj, momentum_up, average_up, grad_up)
    fourth_set = update(up_bias, momentum_bias, average_bias, grad_up_bias)
    fifth_set = update(down_proj, momentum_down, average_down, grad_down)
    sixth_set = update(head_proj, momentum_head, average_head, grad_head)
    seventh_set = update(vectors, momentum_vectors, average_vectors, grad_vectors)
    return (
        loss,
        first_set[0],
        second_set[0],
        third_set[0],
        fourth_set[0],
        fifth_set[0],
        sixth_set[0],
        seventh_set[0],
        first_set[1],
        second_set[1],
        third_set[1],
        fourth_set[1],
        fifth_set[1],
        sixth_set[1],
        seventh_set[1],
        first_set[2],
        second_set[2],
        third_set[2],
        fourth_set[2],
        fifth_set[2],
        sixth_set[2],
        seventh_set[2],
        grad_frames,
    )


def solution(mesh):
    in_specs = (
        P("dp", "tp", None),
        P("dp", "tp", None),
        P("dp", None),
        P("dp", None),
        P(None, None, "tp"),
        P("tp", None),
        P(None, "tp"),
        P("tp"),
        P(None, "tp"),
        P(),
        P(),
        P(None, None, "tp"),
        P("tp", None),
        P(None, "tp"),
        P("tp"),
        P(None, "tp"),
        P(),
        P(),
        P(None, None, "tp"),
        P("tp", None),
        P(None, "tp"),
        P("tp"),
        P(None, "tp"),
        P(),
        P(),
    )
    out_specs = (
        P(),
        P(None, None, "tp"),
        P("tp", None),
        P(None, "tp"),
        P("tp"),
        P(None, "tp"),
        P(),
        P(),
        P(None, None, "tp"),
        P("tp", None),
        P(None, "tp"),
        P("tp"),
        P(None, "tp"),
        P(),
        P(),
        P(None, None, "tp"),
        P("tp", None),
        P(None, "tp"),
        P("tp"),
        P(None, "tp"),
        P(),
        P(),
        P("dp", "tp", None),
    )
    return jax.shard_map(
        per_device, mesh=mesh, in_specs=in_specs, out_specs=out_specs, check_vma=False
    )
```

profile of v0, /device:TPU:0, one launch (start us, length us, event | category | flops | bytes accessed | tf_op | source)
XLA Modules:
  0.0 926.0 jit_solution(6012306189877405584)
XLA Ops:
  14.3 33.5 %all-gather.5.cloned.1.call-done = bf16[2,2304,384]{2,1,0:T(8,128)(2,1)} async-done(((bf16[2,576,384]{2,1,0:T(8,128)(2,1)}), bf16[2,2304,384]{2,1,0:T(8,128)(2,1)}) %all-gather.5.cloned.1.call-update) | async-done | bytes 3538960 | tf_op jit(solution)/shard_map/all_gather | solution.py:121
  61.8 57.2 %while.22 = (s32[]{:T(128)}, bf16[4,2304,48]{1,2,0:T(8,128)(2,1)}, f32[4,2304]{1,0:T(4,128)}, bf16[4,2304,48]{2,1,0:T(8,128)(2,1)S(1)}, bf16[4,2304,48]{2,1,0:T(...) while((s32[]{:T(128)}, bf16[4,2304,48]{1,2,0:T(8,128)(2,1)}, f32[4,2304]{1,0:T(4,128)}, ...), condition=%wide.region_5.6_spmd, body=%wide.region_2.0_spmd.sunk | while | flops 1056483072 | bytes 65804384 | solution.py:124
  61.8 4.0 fusion.141
  68.9 5.8 fusion.143
  76.1 4.0 fusion.141
  83.1 5.8 fusion.143
  90.4 4.0 fusion.141
  97.4 5.8 fusion.143
  104.7 4.0 fusion.141
  111.7 5.8 fusion.143
  119.0 5.8 fusion.97
  124.9 63.7 %reduce-scatter.5.cloned.1.call-done = f32[2,576,384]{2,1,0:T(8,128)} async-done(((f32[2,2304,384]{2,1,0:T(8,128)}), f32[2,576,384]{2,1,0:T(8,128)}) %reduce-scatter.5.cloned.1.call-update) | async-done | bytes 1769488 | tf_op jit(solution)/shard_map/reduce_scatter | solution.py:126
  192.6 30.7 %all-gather.7.cloned.1.call-done = bf16[2,2304,384]{2,1,0:T(8,128)(2,1)} async-done(((bf16[2,576,384]{2,1,0:T(8,128)(2,1)}), bf16[2,2304,384]{2,1,0:T(8,128)(2,1)}) %all-gather.7.cloned.1.call-update) | async-done | bytes 3538960 | tf_op jit(solution)/shard_map/all_gather | solution.py:134
  223.3 4.4 fusion.84
  230.6 4.8 fusion.80
  237.9 61.4 %reduce-scatter.7.cloned.1.call-done = f32[2,576,384]{2,1,0:T(8,128)} async-done(((f32[2,2304,384]{2,1,0:T(8,128)}), f32[2,576,384]{2,1,0:T(8,128)}) %reduce-scatter.7.cloned.1.call-update) | async-done | bytes 1769488 | tf_op jit(solution)/shard_map/reduce_scatter | solution.py:137
  307.0 30.7 %all-gather.9.cloned.1.call-done = bf16[2,2304,384]{2,1,0:T(8,128)(2,1)} async-done(((bf16[2,576,384]{2,1,0:T(8,128)(2,1)}), bf16[2,2304,384]{2,1,0:T(8,128)(2,1)}) %all-gather.9.cloned.1.call-update) | async-done | bytes 3538960 | tf_op jit(solution)/shard_map/all_gather | solution.py:155
  337.7 10.0 %convert_reduce_fusion = (f32[384]{0:T(512)}, bf16[2,2304,384]{2,1,0:T(8,128)(2,1)S(1)}) fusion(f32[2,2304,384]{2,1,0:T(8,128)} %copy-done.17, f32[384]{0:T(512)S(1)} %copy-done.71, bf16[2,2304,384]{2,1,0:T(8,128)(2,1)} %all-gather.9.cloned.1.call-done, f32[384,384]{1,0:T(8,128)} %param.37), kind=kOutput, calls=%fused_computation.64 | convolution fusion | flops 1399799424 | bytes 14748672 | tf_op jit(solution)/shard_map/bsd,df->bsf/dot_general | solution.py:16
  349.5 4.3 fusion.82
  353.9 63.8 %reduce-scatter.9.cloned.1.call-done = f32[2,576,384]{2,1,0:T(8,128)} async-done(((f32[2,2304,384]{2,1,0:T(8,128)}), f32[2,576,384]{2,1,0:T(8,128)}) %reduce-scatter.9.cloned.1.call-update) | async-done | bytes 1769488 | tf_op jit(solution)/shard_map/reduce_scatter | solution.py:161
  427.8 8.2 convolution_bitcast_fusion.1
  438.8 18.2 %all-gather.11.cloned.1.call-done = bf16[2,2304,384]{2,1,0:T(8,128)(2,1)} async-done(((bf16[2,576,384]{2,1,0:T(8,128)(2,1)}), bf16[2,2304,384]{2,1,0:T(8,128)(2,1)}) %all-gather.11.cloned.1.call-update) | async-done | bytes 3538960 | tf_op jit(solution)/shard_map/all_gather | solution.py:172
  463.4 263.5 %while.23 = (s32[]{:T(128)}, bf16[4,3,2304,48]{2,3,1,0:T(8,128)(2,1)}, bf16[4,2304,48]{2,1,0:T(8,128)(2,1)S(1)}, bf16[4,2304,48]{2,1,0:T(8,128)(2,1)}, f32[4,230...) while((s32[]{:T(128)}, ...), condition=%wide.region_17.18_spmd, body=%wide.region_15.17_spmd.sunk | while | flops 2593048320 | bytes 211429520 | solution.py:176
  464.2 11.4 %fusion.152 = f32[2304,2304]{0,1:T(8,128)} fusion(bf16[4,2304,48]{2,1,0:T(8,128)(2,1)} %get-tuple-element.366, s32[]{:T(128)S(6)} %copy.111, bf16[4,2304,48]{2,1,0:T(8,128)(2,1)} %get-tuple-element.365), kind=kOutput, calls=%fused_computation.33.clone.1 | convolution fusion | flops 509607936 | bytes 22414336 | tf_op jit(solution)/shard_map/while/body/eval_jaxpr/qd,kd->qk/dot_general | solution.py:16
  475.7 13.6 %multiply_reduce_fusion.11 = (f32[2304]{0:T(1024)S(1)}, f32[2304,2304]{0,1:T(8,128)}) fusion(f32[2304,2304]{0,1:T(8,128)} %fusion.152, f32[2304]{0:T(1024)S(1)} %dynamic-slice_reduce_fusion.2, bf16[4,2304,48]{2,1,0:T(8,128)(2,1)S(1)} %copy-done.5, s32[]{:T(128)S(6)} %copy.111, bf16[4,2304,48]{2,1,0:T(8,128)(2,1)S(1)} %get-tuple-element.362), kind=kOutput, calls=%fused_computation.20.clone.1 | convolution fusion | flops 530839296 | bytes 43669504 | tf_op jit(solution)/shard_map/while/body/eval_jaxpr/qd,kd->qk/dot_general | solution.py:16
  489.3 18.4 %multiply_convert_fusion.9 = bf16[2304,2304]{0,1:T(8,128)(2,1)} fusion(f32[2304,2304]{0,1:T(8,128)} %get-tuple-element.318, f32[2304,2304]{0,1:T(8,128)} %fusion.152, f32[2304]{0:T(1024)S(1)} %get-tuple-element.319), kind=kLoop, calls=%fused_computation.19.clone.1 | loop fusion | flops 15925248 | bytes 53093376 | tf_op jit(solution)/shard_map/while/body/eval_jaxpr/convert_element_type | solution.py:55
  507.7 10.5 %fusion.153 = bf16[1,1,2304,48]{2,3,1,0:T(8,128)(2,1)S(1)} fusion(f32[2304,2304]{0,1:T(8,128)} %get-tuple-element.318, bf16[4,2304,48]{2,1,0:T(8,128)(2,1)} %get-tuple-element.365, s32[]{:T(128)S(6)} %copy.111), kind=kOutput, calls=%fused_computation.31.clone.1 | convolution fusion | flops 515026944 | bytes 22044676 | tf_op jit(solution)/shard_map/while/body/eval_jaxpr/qk,qd->kd/dot_general | solution.py:16
  518.2 6.2 fusion.155
  530.3 11.4 %fusion.152 = f32[2304,2304]{0,1:T(8,128)} fusion(bf16[4,2304,48]{2,1,0:T(8,128)(2,1)} %get-tuple-element.366, s32[]{:T(128)S(6)} %copy.111, bf16[4,2304,48]{2,1,0:T(8,128)(2,1)} %get-tuple-element.365), kind=kOutput, calls=%fused_computation.33.clone.1 | convolution fusion | flops 509607936 | bytes 22414336 | tf_op jit(solution)/shard_map/while/body/eval_jaxpr/qd,kd->qk/dot_general | solution.py:16
  541.8 13.6 %multiply_reduce_fusion.11 = (f32[2304]{0:T(1024)S(1)}, f32[2304,2304]{0,1:T(8,128)}) fusion(f32[2304,2304]{0,1:T(8,128)} %fusion.152, f32[2304]{0:T(1024)S(1)} %dynamic-slice_reduce_fusion.2, bf16[4,2304,48]{2,1,0:T(8,128)(2,1)S(1)} %copy-done.5, s32[]{:T(128)S(6)} %copy.111, bf16[4,2304,48]{2,1,0:T(8,128)(2,1)S(1)} %get-tuple-element.362), kind=kOutput, calls=%fused_computation.20.clone.1 | convolution fusion | flops 530839296 | bytes 43669504 | tf_op jit(solution)/shard_map/while/body/eval_jaxpr/qd,kd->qk/dot_general | solution.py:16
  555.3 18.4 %multiply_convert_fusion.9 = bf16[2304,2304]{0,1:T(8,128)(2,1)} fusion(f32[2304,2304]{0,1:T(8,128)} %get-tuple-element.318, f32[2304,2304]{0,1:T(8,128)} %fusion.152, f32[2304]{0:T(1024)S(1)} %get-tuple-element.319), kind=kLoop, calls=%fused_computation.19.clone.1 | loop fusion | flops 15925248 | bytes 53093376 | tf_op jit(solution)/shard_map/while/body/eval_jaxpr/convert_element_type | solution.py:55
  573.7 10.5 %fusion.153 = bf16[1,1,2304,48]{2,3,1,0:T(8,128)(2,1)S(1)} fusion(f32[2304,2304]{0,1:T(8,128)} %get-tuple-element.318, bf16[4,2304,48]{2,1,0:T(8,128)(2,1)} %get-tuple-element.365, s32[]{:T(128)S(6)} %copy.111), kind=kOutput, calls=%fused_computation.31.clone.1 | convolution fusion | flops 515026944 | bytes 22044676 | tf_op jit(solution)/shard_map/while/body/eval_jaxpr/qk,qd->kd/dot_general | solution.py:16
  584.2 6.2 fusion.155
  596.2 11.4 %fusion.152 = f32[2304,2304]{0,1:T(8,128)} fusion(bf16[4,2304,48]{2,1,0:T(8,128)(2,1)} %get-tuple-element.366, s32[]{:T(128)S(6)} %copy.111, bf16[4,2304,48]{2,1,0:T(8,128)(2,1)} %get-tuple-element.365), kind=kOutput, calls=%fused_computation.33.clone.1 | convolution fusion | flops 509607936 | bytes 22414336 | tf_op jit(solution)/shard_map/while/body/eval_jaxpr/qd,kd->qk/dot_general | solution.py:16
  607.6 13.5 %multiply_reduce_fusion.11 = (f32[2304]{0:T(1024)S(1)}, f32[2304,2304]{0,1:T(8,128)}) fusion(f32[2304,2304]{0,1:T(8,128)} %fusion.152, f32[2304]{0:T(1024)S(1)} %dynamic-slice_reduce_fusion.2, bf16[4,2304,48]{2,1,0:T(8,128)(2,1)S(1)} %copy-done.5, s32[]{:T(128)S(6)} %copy.111, bf16[4,2304,48]{2,1,0:T(8,128)(2,1)S(1)} %get-tuple-element.362), kind=kOutput, calls=%fused_computation.20.clone.1 | convolution fusion | flops 530839296 | bytes 43669504 | tf_op jit(solution)/shard_map/while/body/eval_jaxpr/qd,kd->qk/dot_general | solution.py:16
  621.2 18.3 %multiply_convert_fusion.9 = bf16[2304,2304]{0,1:T(8,128)(2,1)} fusion(f32[2304,2304]{0,1:T(8,128)} %get-tuple-element.318, f32[2304,2304]{0,1:T(8,128)} %fusion.152, f32[2304]{0:T(1024)S(1)} %get-tuple-element.319), kind=kLoop, calls=%fused_computation.19.clone.1 | loop fusion | flops 15925248 | bytes 53093376 | tf_op jit(solution)/shard_map/while/body/eval_jaxpr/convert_element_type | solution.py:55
  639.5 10.4 %fusion.153 = bf16[1,1,2304,48]{2,3,1,0:T(8,128)(2,1)S(1)} fusion(f32[2304,2304]{0,1:T(8,128)} %get-tuple-element.318, bf16[4,2304,48]{2,1,0:T(8,128)(2,1)} %get-tuple-element.365, s32[]{:T(128)S(6)} %copy.111), kind=kOutput, calls=%fused_computation.31.clone.1 | convolution fusion | flops 515026944 | bytes 22044676 | tf_op jit(solution)/shard_map/while/body/eval_jaxpr/qk,qd->kd/dot_general | solution.py:16
  649.9 6.2 fusion.155
  661.9 11.4 %fusion.152 = f32[2304,2304]{0,1:T(8,128)} fusion(bf16[4,2304,48]{2,1,0:T(8,128)(2,1)} %get-tuple-element.366, s32[]{:T(128)S(6)} %copy.111, bf16[4,2304,48]{2,1,0:T(8,128)(2,1)} %get-tuple-element.365), kind=kOutput, calls=%fused_computation.33.clone.1 | convolution fusion | flops 509607936 | bytes 22414336 | tf_op jit(solution)/shard_map/while/body/eval_jaxpr/qd,kd->qk/dot_general | solution.py:16
  673.3 13.5 %multiply_reduce_fusion.11 = (f32[2304]{0:T(1024)S(1)}, f32[2304,2304]{0,1:T(8,128)}) fusion(f32[2304,2304]{0,1:T(8,128)} %fusion.152, f32[2304]{0:T(1024)S(1)} %dynamic-slice_reduce_fusion.2, bf16[4,2304,48]{2,1,0:T(8,128)(2,1)S(1)} %copy-done.5, s32[]{:T(128)S(6)} %copy.111, bf16[4,2304,48]{2,1,0:T(8,128)(2,1)S(1)} %get-tuple-element.362), kind=kOutput, calls=%fused_computation.20.clone.1 | convolution fusion | flops 530839296 | bytes 43669504 | tf_op jit(solution)/shard_map/while/body/eval_jaxpr/qd,kd->qk/dot_general | solution.py:16
  686.9 18.3 %multiply_convert_fusion.9 = bf16[2304,2304]{0,1:T(8,128)(2,1)} fusion(f32[2304,2304]{0,1:T(8,128)} %get-tuple-element.318, f32[2304,2304]{0,1:T(8,128)} %fusion.152, f32[2304]{0:T(1024)S(1)} %get-tuple-element.319), kind=kLoop, calls=%fused_computation.19.clone.1 | loop fusion | flops 15925248 | bytes 53093376 | tf_op jit(solution)/shard_map/while/body/eval_jaxpr/convert_element_type | solution.py:55
  705.1 10.4 %fusion.153 = bf16[1,1,2304,48]{2,3,1,0:T(8,128)(2,1)S(1)} fusion(f32[2304,2304]{0,1:T(8,128)} %get-tuple-element.318, bf16[4,2304,48]{2,1,0:T(8,128)(2,1)} %get-tuple-element.365, s32[]{:T(128)S(6)} %copy.111), kind=kOutput, calls=%fused_computation.31.clone.1 | convolution fusion | flops 515026944 | bytes 22044676 | tf_op jit(solution)/shard_map/while/body/eval_jaxpr/qk,qd->kd/dot_general | solution.py:16
  715.5 6.2 fusion.155
  733.5 4.9 bitcast_convert_fusion
  744.0 22.1 %psum.60 = f32[384]{0:T(512)S(1)} all-reduce(f32[384]{0:T(512)} %get-tuple-element.228), channel_id=1, replica_groups=mesh['dp'=8,'tp'=4] {'dp'}, use_global_device_ids=true, to_apply=%region_22.23 | all-reduce | flops 384 | bytes 3072 | tf_op jit(solution)/shard_map/psum | solution.py:202
  770.4 58.2 %all-reduce.7.cloned.1.call-done = (f32[3,384,96]{1,2,0:T(8,128)}, f32[96,384]{1,0:T(8,128)}, f32[384,384]{1,0:T(8,128)}, f32[384,384]{1,0:T(8,128)}) async-done(((f32[3,384,96]{1,2,0:T(8,128)}, f32[96,384]{1,0:T(8,128)}, f32[384,384]{1,0:T(8,128)}, f32[384,384]{1,0:T(8,128)}), (f32[3,384,96]{1,2,0:T(8,128)}, f32[96,384]{1,0:T(8,128)}, f32[384,384]{1,0:T(8,128)}, ...) | async-done | bytes 1769488 | tf_op jit(solution)/shard_map/psum | solution.py:202
  836.3 35.0 %reduce-scatter.11.cloned.1.call-done = bf16[2,576,384]{2,1,0:T(8,128)(2,1)} async-done(((bf16[2,2304,384]{2,1,0:T(8,128)(2,1)}), bf16[2,576,384]{2,1,0:T(8,128)(2,1)}) %reduce-scatter.11.cloned.1.call-update) | async-done | bytes 884752 | tf_op jit(solution)/shard_map/reduce_scatter | solution.py:179
  874.8 39.9 %all-reduce = (f32[]{:T(128)}, f32[9,384]{1,0:T(8,128)}) all-reduce(f32[]{:T(128)S(6)} %div.48, f32[9,384]{1,0:T(8,128)S(1)} %stack.61), channel_id=1, replica_groups=mesh['dp'=8,'tp'=4] {'dp','tp'}, use_global_device_ids=true, to_apply=%region_11.12 | all-reduce | flops 3457 | bytes 27656 | tf_op jit(solution)/shard_map/psum | solution.py:205
  (281 shorter events, 131.2 us)
Async XLA Ops:
  7.2 229.1 %copy-start = (bf16[2,576,384]{2,1,0:T(8,128)(2,1)S(1)}, bf16[2,576,384]{2,1,0:T(8,128)(2,1)}, u32[]{:S(2)}) copy-start(bf16[2,576,384]{2,1,0:T(8,128)(2,1)} %param.30) | copy-start | bytes 2654212
  7.2 40.6 %copy-start.41 = (f32[3,384,96]{1,2,0:T(8,128)S(1)}, f32[3,384,96]{1,2,0:T(8,128)}, u32[]{:S(2)}) copy-start(f32[3,384,96]{1,2,0:T(8,128)} %param.33) | copy-start | bytes 1327108
  7.2 40.6 %all-gather.5.cloned.1.call-start = ((), (), s32[]{:S(2)}) async-start(), calls=%async_computation.4 | async-start | bytes 4423680 | tf_op jit(solution)/shard_map/all_gather | solution.py:121
  14.2 174.4 %reduce-scatter.5.cloned.1.call-start = ((), (), s32[]{:S(2)}) async-start(), calls=%async_computation.5 | async-start | bytes 8847360 | tf_op jit(solution)/shard_map/reduce_scatter | solution.py:126
  61.8 57.2 %copy-start.23 = (f32[96,384]{1,0:T(8,128)S(1)}, f32[96,384]{1,0:T(8,128)}, u32[]{:S(2)}) copy-start(f32[96,384]{1,0:T(8,128)} %param.34) | copy-start | bytes 442372
  124.8 63.8 %copy-start.7 = (bf16[2,576,384]{2,1,0:T(8,128)(2,1)S(1)}, bf16[2,576,384]{2,1,0:T(8,128)(2,1)}, u32[]{:S(2)}) copy-start(bf16[2,576,384]{2,1,0:T(8,128)(2,1)} %param.29) | copy-start | bytes 2654212
  124.8 63.8 %copy-start.53 = (f32[384]{0:T(512)S(1)}, f32[384]{0:T(512)}, u32[]{:S(2)}) copy-start(f32[384]{0:T(512)} %get-tuple-element.155) | copy-start | bytes 4612
  124.8 63.8 %copy-start.57 = (f32[384]{0:T(512)S(1)}, f32[384]{0:T(512)}, u32[]{:S(2)}) copy-start(f32[384]{0:T(512)} %get-tuple-element.152) | copy-start | bytes 4612
  124.9 98.4 %all-gather.7.cloned.1.call-start = ((), (), s32[]{:S(2)}) async-start(), calls=%async_computation.6 | async-start | bytes 4423680 | tf_op jit(solution)/shard_map/all_gather | solution.py:134
  190.5 32.7 %copy-start.19 = (f32[384,384]{1,0:T(8,128)S(1)}, f32[384,384]{1,0:T(8,128)}, u32[]{:S(2)}) copy-start(f32[384,384]{1,0:T(8,128)} %param.35) | copy-start | bytes 1769476
  192.4 38.2 %copy-start.71 = (f32[384]{0:T(512)S(1)}, f32[384]{0:T(512)}, u32[]{:S(2)}) copy-start(f32[384]{0:T(512)} %param.36) | copy-start | bytes 4612
  192.4 107.0 %reduce-scatter.7.cloned.1.call-start = ((), (), s32[]{:S(2)}) async-start(), calls=%async_computation.7 | async-start | bytes 8847360 | tf_op jit(solution)/shard_map/reduce_scatter | solution.py:137
  235.4 63.9 %copy-start.55 = (f32[384]{0:T(512)S(1)}, f32[384]{0:T(512)}, u32[]{:S(2)}) copy-start(f32[384]{0:T(512)} %get-tuple-element.148) | copy-start | bytes 4612
  235.4 63.9 %copy-start.56 = (f32[384]{0:T(512)S(1)}, f32[384]{0:T(512)}, u32[]{:S(2)}) copy-start(f32[384]{0:T(512)} %get-tuple-element.151) | copy-start | bytes 4612
  235.4 102.3 %all-gather.9.cloned.1.call-start = ((), (), s32[]{:S(2)}) async-start(), calls=%async_computation.8 | async-start | bytes 4423680 | tf_op jit(solution)/shard_map/all_gather | solution.py:155
  237.9 63.3 %copy-start.21 = (f32[384,384]{1,0:T(8,128)S(1)}, f32[384,384]{1,0:T(8,128)}, u32[]{:S(2)}) copy-start(f32[384,384]{1,0:T(8,128)} %param.38) | copy-start | bytes 1769476
  237.9 63.3 %copy-start.72 = (f32[384]{0:T(512)S(1)}, f32[384]{0:T(512)}, u32[]{:S(2)}) copy-start(f32[384]{0:T(512)} %get-tuple-element.147) | copy-start | bytes 4612
  306.8 110.9 %reduce-scatter.9.cloned.1.call-start = ((), (), s32[]{:S(2)}) async-start(), calls=%async_computation.9 | async-start | bytes 8847360 | tf_op jit(solution)/shard_map/reduce_scatter | solution.py:161
  353.8 103.2 %all-gather.11.cloned.1.call-start = ((), (), s32[]{:S(2)}) async-start(), calls=%async_computation.10 | async-start | bytes 4423680 | tf_op jit(solution)/shard_map/all_gather | solution.py:172
  426.1 315.3 %all-reduce.5.cloned.1.call-start = ((), (), s32[]{:S(2)}) async-start(), calls=%async_computation.11 | async-start | bytes 1179648 | tf_op jit(solution)/shard_map/psum | solution.py:205
  427.7 400.9 %all-reduce.7.cloned.1.call-start = ((), (), s32[]{:S(2)}) async-start(), calls=%async_computation.13 | async-start | bytes 3538944 | tf_op jit(solution)/shard_map/psum | solution.py:202
  436.0 21.1 %copy-start.24 = (f32[96,384]{1,0:T(8,128)S(1)}, f32[96,384]{1,0:T(8,128)}, u32[]{:S(2)}) copy-start(f32[96,384]{1,0:T(8,128)} %param.34) | copy-start | bytes 442372
  464.2 11.4 %copy-start.5 = (bf16[4,2304,48]{2,1,0:T(8,128)(2,1)S(1)}, bf16[4,2304,48]{2,1,0:T(8,128)(2,1)}, u32[]{:S(2)}) copy-start(bf16[4,2304,48]{2,1,0:T(8,128)(2,1)} %get-tuple-element.363) | copy-start | bytes 2654212 | tf_op jit(solution)/shard_map/while
  733.5 137.8 %reduce-scatter.11.cloned.1.call-start = ((), (), s32[]{:S(2)}) async-start(), calls=%async_computation.12 | async-start | bytes 4423680 | tf_op jit(solution)/shard_map/reduce_scatter | solution.py:179
  738.4 29.0 %copy-start.62 = (f32[384]{0:T(512)S(1)}, f32[384]{0:T(512)}, u32[]{:S(2)}) copy-start(f32[384]{0:T(512)} %get-tuple-element.135) | copy-start | bytes 4612
  738.5 29.6 %copy-start.61 = (f32[384]{0:T(512)S(1)}, f32[384]{0:T(512)}, u32[]{:S(2)}) copy-start(f32[384]{0:T(512)} %get-tuple-element.142) | copy-start | bytes 4612
  738.5 31.4 %copy-start.63 = (f32[384]{0:T(512)S(1)}, f32[384]{0:T(512)}, u32[]{:S(2)}) copy-start(f32[384]{0:T(512)} %get-tuple-element.144) | copy-start | bytes 4612
  738.5 90.1 %copy-start.25 = (f32[96,384]{1,0:T(8,128)S(1)}, f32[96,384]{1,0:T(8,128)}, u32[]{:S(2)}) copy-start(f32[96,384]{1,0:T(8,128)} %param.34) | copy-start | bytes 442372
  738.5 90.1 %copy-start.45 = (f32[96,384]{1,0:T(8,128)S(1)}, f32[96,384]{1,0:T(8,128)}, u32[]{:S(2)}) copy-start(f32[96,384]{1,0:T(8,128)} %param.48) | copy-start | bytes 442372
  738.5 90.1 %copy-start.46 = (f32[96,384]{1,0:T(8,128)S(1)}, f32[96,384]{1,0:T(8,128)}, u32[]{:S(2)}) copy-start(f32[96,384]{1,0:T(8,128)} %param.41) | copy-start | bytes 442372
  741.4 89.0 %copy-start.42 = (f32[3,384,96]{1,2,0:T(8,128)S(1)}, f32[3,384,96]{1,2,0:T(8,128)}, u32[]{:S(2)}) copy-start(f32[3,384,96]{1,2,0:T(8,128)} %param.33) | copy-start | bytes 1327108
  741.4 89.0 %copy-start.43 = (f32[3,384,96]{1,2,0:T(8,128)S(1)}, f32[3,384,96]{1,2,0:T(8,128)}, u32[]{:S(2)}) copy-start(f32[3,384,96]{1,2,0:T(8,128)} %param.47) | copy-start | bytes 1327108
  741.4 89.0 %copy-start.44 = (f32[3,384,96]{1,2,0:T(8,128)S(1)}, f32[3,384,96]{1,2,0:T(8,128)}, u32[]{:S(2)}) copy-start(f32[3,384,96]{1,2,0:T(8,128)} %param.40) | copy-start | bytes 1327108
  744.0 88.6 %copy-start.20 = (f32[384,384]{1,0:T(8,128)S(1)}, f32[384,384]{1,0:T(8,128)}, u32[]{:S(2)}) copy-start(f32[384,384]{1,0:T(8,128)} %param.35) | copy-start | bytes 1769476
  744.0 88.6 %copy-start.33 = (f32[384,384]{1,0:T(8,128)S(1)}, f32[384,384]{1,0:T(8,128)}, u32[]{:S(2)}) copy-start(f32[384,384]{1,0:T(8,128)} %param.49) | copy-start | bytes 1769476
  744.0 88.6 %copy-start.34 = (f32[384,384]{1,0:T(8,128)S(1)}, f32[384,384]{1,0:T(8,128)}, u32[]{:S(2)}) copy-start(f32[384,384]{1,0:T(8,128)} %param.42) | copy-start | bytes 1769476
  834.1 37.2 %copy-start.8 = (bf16[2,576,384]{2,1,0:T(8,128)(2,1)S(1)}, bf16[2,576,384]{2,1,0:T(8,128)(2,1)}, u32[]{:S(2)}) copy-start(bf16[2,576,384]{2,1,0:T(8,128)(2,1)} %param.29) | copy-start | bytes 2654212
  834.1 37.2 %copy-start.48 = (f32[2,576]{1,0:T(2,128)S(1)}, f32[2,576]{1,0:T(2,128)}, u32[]{:S(2)}) copy-start(f32[2,576]{1,0:T(2,128)} %copy-done.47) | copy-start | bytes 13828
  834.1 37.2 %copy-start.50 = (f32[2,576]{1,0:T(2,128)S(1)}, f32[2,576]{1,0:T(2,128)}, u32[]{:S(2)}) copy-start(f32[2,576]{1,0:T(2,128)} %copy-done.49) | copy-start | bytes 13828
  834.1 37.2 %copy-start.52 = (f32[384]{0:T(512)S(1)}, f32[384]{0:T(512)}, u32[]{:S(2)}) copy-start(f32[384]{0:T(512)} %copy-done.51) | copy-start | bytes 4612
  834.8 39.3 %copy-start.64 = (f32[1,384]{1,0:T(1,128)S(1)}, f32[1,384]{1,0:T(1,128)}, u32[]{:S(2)}) copy-start(f32[1,384]{1,0:T(1,128)} %stack.60) | copy-start | bytes 4612
  834.8 39.3 %copy-start.65 = (f32[1,384]{1,0:T(1,128)S(1)}, f32[1,384]{1,0:T(1,128)}, u32[]{:S(2)}) copy-start(f32[1,384]{1,0:T(1,128)} %stack.59) | copy-start | bytes 4612
  834.8 39.3 %copy-start.66 = (f32[1,384]{1,0:T(1,128)S(1)}, f32[1,384]{1,0:T(1,128)}, u32[]{:S(2)}) copy-start(f32[1,384]{1,0:T(1,128)} %stack.58) | copy-start | bytes 4612
  834.8 39.3 %copy-start.67 = (f32[1,384]{1,0:T(1,128)S(1)}, f32[1,384]{1,0:T(1,128)}, u32[]{:S(2)}) copy-start(f32[1,384]{1,0:T(1,128)} %stack.56) | copy-start | bytes 4612
  834.8 39.3 %copy-start.68 = (f32[1,384]{1,0:T(1,128)S(1)}, f32[1,384]{1,0:T(1,128)}, u32[]{:S(2)}) copy-start(f32[1,384]{1,0:T(1,128)} %stack.57) | copy-start | bytes 4612
  834.9 39.3 %copy-start.69 = (f32[1,384]{1,0:T(1,128)S(1)}, f32[1,384]{1,0:T(1,128)}, u32[]{:S(2)}) copy-start(f32[1,384]{1,0:T(1,128)} %stack.55) | copy-start | bytes 4612
  834.9 39.3 %copy-start.70 = (f32[1,384]{1,0:T(1,128)S(1)}, f32[1,384]{1,0:T(1,128)}, u32[]{:S(2)}) copy-start(f32[1,384]{1,0:T(1,128)} %stack.54) | copy-start | bytes 4612
  834.9 81.3 %copy-start.13 = (f32[2,576,384]{2,1,0:T(8,128)S(1)}, f32[2,576,384]{2,1,0:T(8,128)}, u32[]{:S(2)}) copy-start(f32[2,576,384]{2,1,0:T(8,128)} %copy-done.12) | copy-start | bytes 5308420
  (45 other events, 172.4 us)
Sparse Core Ops, SparseCore 0:
  14.4 33.4 all-gather.4
  125.0 63.6 reduce-scatter.4
  192.5 30.7 all-gather.6
  235.6 63.7 reduce-scatter.6
  306.9 30.7 all-gather.8
  353.9 63.6 reduce-scatter.8
  426.3 30.7 all-gather.10
  463.7 127.3 all-reduce.4
  733.6 95.0 all-reduce.6
  831.2 40.0 reduce-scatter.10
where the time goes:
time: 936 us; the launch traced here: 926 us
  waiting for transfers between devices  396 us (42%)
  matrix products  282 us (30%)
  other arithmetic  126 us (13%)
  blocking collectives  62 us (7%)
  local copies, waits for them, and re-layouts  44 us (5%)
  between operations  15.7 us (2%)
    dot_general x43, matrix products, product(): return jnp.einsum(form, left, right, preferred_element_type=jnp.float32)  282 us
    convert_element_type x4, other arithmetic, head_backward(): grad_scores = (probs * (grad_probs - jnp.sum(probs * grad_probs, axis=-1,...  73.3 us
    reduce_scatter x1, waiting for transfers between devices, per_device(): lax.psum_scatter(product(grad_pre, up_all, 'bsf,df->bsd'), 'tp', scatter_...  63.8 us
    reduce_scatter x1, waiting for transfers between devices, per_device(): lax.psum_scatter(product(attended, out_low, 'bse,ed->bsd'), 'tp', scatter...  63.7 us
    reduce_scatter x1, waiting for transfers between devices, per_device(): lax.psum_scatter(product(hidden, down_all, 'bsf,df->bsd'), 'tp', scatter_...  61.4 us
    psum x1, waiting for transfers between devices, per_device(): lax.psum((grad_attn_proj, grad_out, grad_up, grad_up_bias, grad_down), 'dp')  58.2 us
    psum x1, blocking collectives, per_device(): lax.psum((grad_head, grad_vectors, part_loss), ('dp', 'tp'))  39.9 us
    reduce_scatter x1, waiting for transfers between devices, per_device(): lax.psum_scatter(product(grad_packed, attn_low, 'jbse,jde->bsd').astype(j...  35 us
  transfers between devices with their start and end apart: 10, of which 9 were waited for; matrix products, arithmetic and copies ran while one was open for 33% of the time, Pallas kernels for 0%

commit v1 on v0

--- a/solution.py
+++ b/solution.py
@@ -10,6 +10,27 @@
 MOMENTUM_RATE = 0.9
 LEARN_RATE = 0.02
 AVERAGE_RATE = 0.9
+
+
+def ring_gather(array, axis, dim):
+    size, index, width = (lax.axis_size(axis), lax.axis_index(axis), array.shape[dim])
+    right = [(i, (i + 1) % size) for i in range(size)]
+    left = [(i, (i - 1) % size) for i in range(size)]
+    whole = jnp.zeros((*array.shape[:dim], size * width, *array.shape[dim + 1 :]), array.dtype)
+    whole = lax.dynamic_update_slice_in_dim(whole, array, index * width, axis=dim)
+    from_left = from_right = array
+    half = size // 2
+    for step in range(1, half + 1):
+        from_left = lax.ppermute(from_left, axis, right)
+        whole = lax.dynamic_update_slice_in_dim(
+            whole, from_left, (index - step) % size * width, axis=dim
+        )
+        if step < size - half:
+            from_right = lax.ppermute(from_right, axis, left)
+            whole = lax.dynamic_update_slice_in_dim(
+                whole, from_right, (index + step) % size * width, axis=dim
+            )
+    return whole
 
 
 def product(left, right, form):
@@ -131,7 +152,7 @@
     second_low = second.astype(bf16)
     up_all = up_proj.astype(bf16)
     down_all = down_proj.astype(bf16)
-    second_all = lax.all_gather(second_low, "tp", axis=1, tiled=True)
+    second_all = ring_gather(second_low, "tp", 1)
     hidden_pre = product(second_all, up_all, "bsd,df->bsf") + up_bias
     hidden = jax.nn.gelu(hidden_pre).astype(bf16)
     ffn_term = lax.psum_scatter(

time: 936 us -> 983 us (1.050)
  local copies, waits for them, and re-layouts: 44 us -> 98.4 us
  waiting for transfers between devices: 396 us -> 382 us
    dynamic_update_slice x0 -> x4, local copies, waits for them, and re-layouts: none -> 43.4 us  [the longest x2 21.3 us: ring_gather(): lax.dynamic_update_slice_in_dim(whole, from_left, (index - step) % size *...]
    all_gather x1 -> x0, waiting for transfers between devices: 30.7 us -> none  [per_device(): second_all = lax.all_gather(second_low, 'tp', axis=1, tiled=True)]
    ppermute x0 -> x3, waiting for transfers between devices: none -> 19.7 us  [the longest x2 19.7 us: ring_gather(): from_left = lax.ppermute(from_left, axis, right)]
  transfers between devices with their start and end apart: 10 -> 12, of which waited for: 9 -> 9; matrix products, arithmetic and copies ran while one was open for 33% -> 36% of each run, Pallas kernels for 0% -> 0%
where the time goes in v1:
time: 983 us; the launch traced here: 971 us
  waiting for transfers between devices  382 us (39%)
  matrix products  284 us (29%)
  other arithmetic  126 us (13%)
  local copies, waits for them, and re-layouts  98.4 us (10%)
  blocking collectives  61.9 us (6%)
  between operations  15.5 us (2%)
    dot_general x43, matrix products, product(): return jnp.einsum(form, left, right, preferred_element_type=jnp.float32)  284 us
    convert_element_type x4, other arithmetic, head_backward(): grad_scores = (probs * (grad_probs - jnp.sum(probs * grad_probs, axis=-1,...  73.3 us
    reduce_scatter x1, waiting for transfers between devices, per_device(): lax.psum_scatter(product(attended, out_low, 'bse,ed->bsd'), 'tp', scatter...  63.8 us
    reduce_scatter x1, waiting for transfers between devices, per_device(): lax.psum_scatter(product(grad_pre, up_all, 'bsf,df->bsd'), 'tp', scatter_...  63.8 us
    reduce_scatter x1, waiting for transfers between devices, per_device(): lax.psum_scatter(product(hidden, down_all, 'bsf,df->bsd'), 'tp', scatter_...  62.2 us
    psum x1, waiting for transfers between devices, per_device(): lax.psum((grad_attn_proj, grad_out, grad_up, grad_up_bias, grad_down), 'dp')  57.3 us
    psum x1, blocking collectives, per_device(): lax.psum((grad_head, grad_vectors, part_loss), ('dp', 'tp'))  39.9 us
    reduce_scatter x1, waiting for transfers between devices, per_device(): lax.psum_scatter(product(grad_packed, attn_low, 'jbse,jde->bsd').astype(j...  35.2 us
  transfers between devices with their start and end apart: 12, of which 9 were waited for; matrix products, arithmetic and copies ran while one was open for 36% of the time, Pallas kernels for 0%

profile of v1, /device:TPU:0, one launch (start us, length us, event | category | flops | bytes accessed | tf_op | source)
XLA Modules:
  0.0 971.3 jit_solution(814647472654936825)
XLA Ops:
  15.5 33.5 %all-gather.4.cloned.1.call-done = bf16[2,2304,384]{2,1,0:T(8,128)(2,1)} async-done(((bf16[2,576,384]{2,1,0:T(8,128)(2,1)}), bf16[2,2304,384]{2,1,0:T(8,128)(2,1)}) %all-gather.4.cloned.1.call-update) | async-done | bytes 3538960 | tf_op jit(solution)/shard_map/all_gather | solution.py:142
  62.9 57.2 %while.22 = (s32[]{:T(128)}, bf16[4,2304,48]{1,2,0:T(8,128)(2,1)}, f32[4,2304]{1,0:T(4,128)}, bf16[4,2304,48]{2,1,0:T(8,128)(2,1)S(1)}, bf16[4,2304,48]{2,1,0:T(...) while((s32[]{:T(128)}, bf16[4,2304,48]{1,2,0:T(8,128)(2,1)}, f32[4,2304]{1,0:T(4,128)}, ...), condition=%wide.region_5.6_spmd, body=%wide.region_2.0_spmd.sunk | while | flops 1056483072 | bytes 65804384 | solution.py:145
  70.0 5.8 fusion.143
  84.3 5.8 fusion.143
  98.6 5.8 fusion.143
  112.9 5.8 fusion.143
  120.2 5.8 fusion.97
  126.1 63.8 %reduce-scatter.5.cloned.1.call-done = f32[2,576,384]{2,1,0:T(8,128)} async-done(((f32[2,2304,384]{2,1,0:T(8,128)}), f32[2,576,384]{2,1,0:T(8,128)}) %reduce-scatter.5.cloned.1.call-update) | async-done | bytes 1769488 | tf_op jit(solution)/shard_map/reduce_scatter | solution.py:147
  194.5 19.7 %collective-permute-done = bf16[2,576,384]{2,1,0:T(8,128)(2,1)} collective-permute-done((bf16[2,576,384]{2,1,0:T(8,128)(2,1)S(1)}, bf16[2,576,384]{2,1,0:T(8,128)(2,1)}, u32[]{:S(2)}, u32[]{:S(2)}) %collective-permute-start) | collective-permute-done | bytes 884768 | tf_op jit(solution)/shard_map/ppermute | solution.py:24
  217.7 10.4 %dynamic_update_slice.24 = bf16[2,2304,384]{1,2,0:T(8,128)(2,1)} dynamic-update-slice(bf16[2,2304,384]{1,2,0:T(8,128)(2,1)} %broadcast_in_dim.32, bf16[2,576,384]{1,2,0:T(8,128)(2,1)} %copy.96, s32[]{:T(128)} %copy.146, s32[]{:T(128)S(6)} %select_n.47, s32[]{:T(128)} %copy.146) | dynamic-update-slice | bytes 1769476 | tf_op jit(solution)/shard_map/dynamic_update_slice | solution.py:20
  230.4 10.9 %dynamic_update_slice.25 = bf16[2,2304,384]{1,2,0:T(8,128)(2,1)} dynamic-update-slice(bf16[2,2304,384]{1,2,0:T(8,128)(2,1)} %dynamic_update_slice.24, bf16[2,576,384]{1,2,0:T(8,128)(2,1)} %copy.97, s32[]{:T(128)} %copy.146, s32[]{:T(128)S(6)} %select_n.49, s32[]{:T(128)} %copy.146) | dynamic-update-slice | bytes 1769476 | tf_op jit(solution)/shard_map/dynamic_update_slice | solution.py:25
  243.6 11.6 %dynamic_update_slice.26 = bf16[2,2304,384]{1,2,0:T(8,128)(2,1)} dynamic-update-slice(bf16[2,2304,384]{1,2,0:T(8,128)(2,1)} %dynamic_update_slice.25, bf16[2,576,384]{1,2,0:T(8,128)(2,1)} %copy.98, s32[]{:T(128)} %copy.146, s32[]{:T(128)S(6)} %select_n.51, s32[]{:T(128)} %copy.146) | dynamic-update-slice | bytes 1769476 | tf_op jit(solution)/shard_map/dynamic_update_slice | solution.py:30
  257.4 10.4 %dynamic_update_slice.27 = bf16[2,2304,384]{1,2,0:T(8,128)(2,1)} dynamic-update-slice(bf16[2,2304,384]{1,2,0:T(8,128)(2,1)} %dynamic_update_slice.26, bf16[2,576,384]{1,2,0:T(8,128)(2,1)} %copy.99, s32[]{:T(128)} %copy.146, s32[]{:T(128)S(6)} %select_n.53, s32[]{:T(128)} %copy.146) | dynamic-update-slice | bytes 1769476 | tf_op jit(solution)/shard_map/dynamic_update_slice | solution.py:25
  267.8 4.4 fusion.84
  275.2 4.9 fusion.80
  282.5 62.2 %reduce-scatter.7.cloned.1.call-done = f32[2,576,384]{2,1,0:T(8,128)} async-done(((f32[2,2304,384]{2,1,0:T(8,128)}), f32[2,576,384]{2,1,0:T(8,128)}) %reduce-scatter.7.cloned.1.call-update) | async-done | bytes 1769488 | tf_op jit(solution)/shard_map/reduce_scatter | solution.py:158
  352.5 30.7 %all-gather.6.cloned.1.call-done = bf16[2,2304,384]{2,1,0:T(8,128)(2,1)} async-done(((bf16[2,576,384]{2,1,0:T(8,128)(2,1)}), bf16[2,2304,384]{2,1,0:T(8,128)(2,1)}) %all-gather.6.cloned.1.call-update) | async-done | bytes 3538960 | tf_op jit(solution)/shard_map/all_gather | solution.py:176
  383.1 10.0 %convert_reduce_fusion = (f32[384]{0:T(512)}, bf16[2,2304,384]{2,1,0:T(8,128)(2,1)S(1)}) fusion(f32[2,2304,384]{2,1,0:T(8,128)} %copy-done.13, f32[384]{0:T(512)S(1)} %copy-done.70, bf16[2,2304,384]{2,1,0:T(8,128)(2,1)} %all-gather.6.cloned.1.call-done, f32[384,384]{1,0:T(8,128)} %param.37), kind=kOutput, calls=%fused_computation.64 | convolution fusion | flops 1399799424 | bytes 14748672 | tf_op jit(solution)/shard_map/bsd,df->bsf/dot_general | solution.py:37
  399.3 63.8 %reduce-scatter.9.cloned.1.call-done = f32[2,576,384]{2,1,0:T(8,128)} async-done(((f32[2,2304,384]{2,1,0:T(8,128)}), f32[2,576,384]{2,1,0:T(8,128)}) %reduce-scatter.9.cloned.1.call-update) | async-done | bytes 1769488 | tf_op jit(solution)/shard_map/reduce_scatter | solution.py:182
  473.2 6.0 convolution_bitcast_fusion.2
  479.2 7.6 convolution_bitcast_fusion.1
  486.8 15.7 %all-gather.8.cloned.1.call-done = bf16[2,2304,384]{2,1,0:T(8,128)(2,1)} async-done(((bf16[2,576,384]{2,1,0:T(8,128)(2,1)}), bf16[2,2304,384]{2,1,0:T(8,128)(2,1)}) %all-gather.8.cloned.1.call-update) | async-done | bytes 3538960 | tf_op jit(solution)/shard_map/all_gather | solution.py:193
  508.9 263.6 %while.23 = (s32[]{:T(128)}, bf16[4,3,2304,48]{2,3,1,0:T(8,128)(2,1)}, bf16[4,2304,48]{2,1,0:T(8,128)(2,1)S(1)}, bf16[4,2304,48]{2,1,0:T(8,128)(2,1)}, f32[4,230...) while((s32[]{:T(128)}, ...), condition=%wide.region_17.18_spmd, body=%wide.region_15.17_spmd.sunk | while | flops 2593048320 | bytes 211429520 | solution.py:197
  509.7 11.4 %fusion.152 = f32[2304,2304]{0,1:T(8,128)} fusion(bf16[4,2304,48]{2,1,0:T(8,128)(2,1)} %get-tuple-element.366, s32[]{:T(128)S(6)} %copy.136, bf16[4,2304,48]{2,1,0:T(8,128)(2,1)} %get-tuple-element.365), kind=kOutput, calls=%fused_computation.33.clone.1 | convolution fusion | flops 509607936 | bytes 22414336 | tf_op jit(solution)/shard_map/while/body/eval_jaxpr/qd,kd->qk/dot_general | solution.py:37
  521.1 13.7 %multiply_reduce_fusion.11 = (f32[2304]{0:T(1024)S(1)}, f32[2304,2304]{0,1:T(8,128)}) fusion(f32[2304,2304]{0,1:T(8,128)} %fusion.152, f32[2304]{0:T(1024)S(1)} %dynamic-slice_reduce_fusion.2, bf16[4,2304,48]{2,1,0:T(8,128)(2,1)S(1)} %copy-done.5, s32[]{:T(128)S(6)} %copy.136, bf16[4,2304,48]{2,1,0:T(8,128)(2,1)S(1)} %get-tuple-element.362), kind=kOutput, calls=%fused_computation.20.clone.1 | convolution fusion | flops 530839296 | bytes 43669504 | tf_op jit(solution)/shard_map/while/body/eval_jaxpr/qd,kd->qk/dot_general | solution.py:37
  534.8 18.4 %multiply_convert_fusion.9 = bf16[2304,2304]{0,1:T(8,128)(2,1)} fusion(f32[2304,2304]{0,1:T(8,128)} %get-tuple-element.318, f32[2304,2304]{0,1:T(8,128)} %fusion.152, f32[2304]{0:T(1024)S(1)} %get-tuple-element.319), kind=kLoop, calls=%fused_computation.19.clone.1 | loop fusion | flops 15925248 | bytes 53093376 | tf_op jit(solution)/shard_map/while/body/eval_jaxpr/convert_element_type | solution.py:76
  553.2 10.5 %fusion.153 = bf16[1,1,2304,48]{2,3,1,0:T(8,128)(2,1)S(1)} fusion(f32[2304,2304]{0,1:T(8,128)} %get-tuple-element.318, bf16[4,2304,48]{2,1,0:T(8,128)(2,1)} %get-tuple-element.365, s32[]{:T(128)S(6)} %copy.136), kind=kOutput, calls=%fused_computation.31.clone.1 | convolution fusion | flops 515026944 | bytes 22044676 | tf_op jit(solution)/shard_map/while/body/eval_jaxpr/qk,qd->kd/dot_general | solution.py:37
  563.7 6.2 fusion.155
  575.8 11.4 %fusion.152 = f32[2304,2304]{0,1:T(8,128)} fusion(bf16[4,2304,48]{2,1,0:T(8,128)(2,1)} %get-tuple-element.366, s32[]{:T(128)S(6)} %copy.136, bf16[4,2304,48]{2,1,0:T(8,128)(2,1)} %get-tuple-element.365), kind=kOutput, calls=%fused_computation.33.clone.1 | convolution fusion | flops 509607936 | bytes 22414336 | tf_op jit(solution)/shard_map/while/body/eval_jaxpr/qd,kd->qk/dot_general | solution.py:37
  587.2 13.6 %multiply_reduce_fusion.11 = (f32[2304]{0:T(1024)S(1)}, f32[2304,2304]{0,1:T(8,128)}) fusion(f32[2304,2304]{0,1:T(8,128)} %fusion.152, f32[2304]{0:T(1024)S(1)} %dynamic-slice_reduce_fusion.2, bf16[4,2304,48]{2,1,0:T(8,128)(2,1)S(1)} %copy-done.5, s32[]{:T(128)S(6)} %copy.136, bf16[4,2304,48]{2,1,0:T(8,128)(2,1)S(1)} %get-tuple-element.362), kind=kOutput, calls=%fused_computation.20.clone.1 | convolution fusion | flops 530839296 | bytes 43669504 | tf_op jit(solution)/shard_map/while/body/eval_jaxpr/qd,kd->qk/dot_general | solution.py:37
  600.8 18.4 %multiply_convert_fusion.9 = bf16[2304,2304]{0,1:T(8,128)(2,1)} fusion(f32[2304,2304]{0,1:T(8,128)} %get-tuple-element.318, f32[2304,2304]{0,1:T(8,128)} %fusion.152, f32[2304]{0:T(1024)S(1)} %get-tuple-element.319), kind=kLoop, calls=%fused_computation.19.clone.1 | loop fusion | flops 15925248 | bytes 53093376 | tf_op jit(solution)/shard_map/while/body/eval_jaxpr/convert_element_type | solution.py:76
  619.2 10.5 %fusion.153 = bf16[1,1,2304,48]{2,3,1,0:T(8,128)(2,1)S(1)} fusion(f32[2304,2304]{0,1:T(8,128)} %get-tuple-element.318, bf16[4,2304,48]{2,1,0:T(8,128)(2,1)} %get-tuple-element.365, s32[]{:T(128)S(6)} %copy.136), kind=kOutput, calls=%fused_computation.31.clone.1 | convolution fusion | flops 515026944 | bytes 22044676 | tf_op jit(solution)/shard_map/while/body/eval_jaxpr/qk,qd->kd/dot_general | solution.py:37
  629.7 6.2 fusion.155
  641.8 11.4 %fusion.152 = f32[2304,2304]{0,1:T(8,128)} fusion(bf16[4,2304,48]{2,1,0:T(8,128)(2,1)} %get-tuple-element.366, s32[]{:T(128)S(6)} %copy.136, bf16[4,2304,48]{2,1,0:T(8,128)(2,1)} %get-tuple-element.365), kind=kOutput, calls=%fused_computation.33.clone.1 | convolution fusion | flops 509607936 | bytes 22414336 | tf_op jit(solution)/shard_map/while/body/eval_jaxpr/qd,kd->qk/dot_general | solution.py:37
  653.2 13.5 %multiply_reduce_fusion.11 = (f32[2304]{0:T(1024)S(1)}, f32[2304,2304]{0,1:T(8,128)}) fusion(f32[2304,2304]{0,1:T(8,128)} %fusion.152, f32[2304]{0:T(1024)S(1)} %dynamic-slice_reduce_fusion.2, bf16[4,2304,48]{2,1,0:T(8,128)(2,1)S(1)} %copy-done.5, s32[]{:T(128)S(6)} %copy.136, bf16[4,2304,48]{2,1,0:T(8,128)(2,1)S(1)} %get-tuple-element.362), kind=kOutput, calls=%fused_computation.20.clone.1 | convolution fusion | flops 530839296 | bytes 43669504 | tf_op jit(solution)/shard_map/while/body/eval_jaxpr/qd,kd->qk/dot_general | solution.py:37
  666.7 18.3 %multiply_convert_fusion.9 = bf16[2304,2304]{0,1:T(8,128)(2,1)} fusion(f32[2304,2304]{0,1:T(8,128)} %get-tuple-element.318, f32[2304,2304]{0,1:T(8,128)} %fusion.152, f32[2304]{0:T(1024)S(1)} %get-tuple-element.319), kind=kLoop, calls=%fused_computation.19.clone.1 | loop fusion | flops 15925248 | bytes 53093376 | tf_op jit(solution)/shard_map/while/body/eval_jaxpr/convert_element_type | solution.py:76
  685.0 10.4 %fusion.153 = bf16[1,1,2304,48]{2,3,1,0:T(8,128)(2,1)S(1)} fusion(f32[2304,2304]{0,1:T(8,128)} %get-tuple-element.318, bf16[4,2304,48]{2,1,0:T(8,128)(2,1)} %get-tuple-element.365, s32[]{:T(128)S(6)} %copy.136), kind=kOutput, calls=%fused_computation.31.clone.1 | convolution fusion | flops 515026944 | bytes 22044676 | tf_op jit(solution)/shard_map/while/body/eval_jaxpr/qk,qd->kd/dot_general | solution.py:37
  695.4 6.2 fusion.155
  707.4 11.4 %fusion.152 = f32[2304,2304]{0,1:T(8,128)} fusion(bf16[4,2304,48]{2,1,0:T(8,128)(2,1)} %get-tuple-element.366, s32[]{:T(128)S(6)} %copy.136, bf16[4,2304,48]{2,1,0:T(8,128)(2,1)} %get-tuple-element.365), kind=kOutput, calls=%fused_computation.33.clone.1 | convolution fusion | flops 509607936 | bytes 22414336 | tf_op jit(solution)/shard_map/while/body/eval_jaxpr/qd,kd->qk/dot_general | solution.py:37
  718.9 13.5 %multiply_reduce_fusion.11 = (f32[2304]{0:T(1024)S(1)}, f32[2304,2304]{0,1:T(8,128)}) fusion(f32[2304,2304]{0,1:T(8,128)} %fusion.152, f32[2304]{0:T(1024)S(1)} %dynamic-slice_reduce_fusion.2, bf16[4,2304,48]{2,1,0:T(8,128)(2,1)S(1)} %copy-done.5, s32[]{:T(128)S(6)} %copy.136, bf16[4,2304,48]{2,1,0:T(8,128)(2,1)S(1)} %get-tuple-element.362), kind=kOutput, calls=%fused_computation.20.clone.1 | convolution fusion | flops 530839296 | bytes 43669504 | tf_op jit(solution)/shard_map/while/body/eval_jaxpr/qd,kd->qk/dot_general | solution.py:37
  732.4 18.3 %multiply_convert_fusion.9 = bf16[2304,2304]{0,1:T(8,128)(2,1)} fusion(f32[2304,2304]{0,1:T(8,128)} %get-tuple-element.318, f32[2304,2304]{0,1:T(8,128)} %fusion.152, f32[2304]{0:T(1024)S(1)} %get-tuple-element.319), kind=kLoop, calls=%fused_computation.19.clone.1 | loop fusion | flops 15925248 | bytes 53093376 | tf_op jit(solution)/shard_map/while/body/eval_jaxpr/convert_element_type | solution.py:76
  750.7 10.4 %fusion.153 = bf16[1,1,2304,48]{2,3,1,0:T(8,128)(2,1)S(1)} fusion(f32[2304,2304]{0,1:T(8,128)} %get-tuple-element.318, bf16[4,2304,48]{2,1,0:T(8,128)(2,1)} %get-tuple-element.365, s32[]{:T(128)S(6)} %copy.136), kind=kOutput, calls=%fused_computation.31.clone.1 | convolution fusion | flops 515026944 | bytes 22044676 | tf_op jit(solution)/shard_map/while/body/eval_jaxpr/qk,qd->kd/dot_general | solution.py:37
  761.1 6.2 fusion.155
  779.0 4.9 bitcast_convert_fusion
  789.8 21.9 %psum.60 = f32[384]{0:T(512)S(1)} all-reduce(f32[384]{0:T(512)} %get-tuple-element.228), channel_id=1, replica_groups=mesh['dp'=8,'tp'=4] {'dp'}, use_global_device_ids=true, to_apply=%region_22.23 | all-reduce | flops 384 | bytes 3072 | tf_op jit(solution)/shard_map/psum | solution.py:223
  816.7 57.3 %all-reduce.7.cloned.1.call-done = (f32[3,384,96]{1,2,0:T(8,128)}, f32[96,384]{1,0:T(8,128)}, f32[384,384]{1,0:T(8,128)}, f32[384,384]{1,0:T(8,128)}) async-done(((f32[3,384,96]{1,2,0:T(8,128)}, f32[96,384]{1,0:T(8,128)}, f32[384,384]{1,0:T(8,128)}, f32[384,384]{1,0:T(8,128)}), (f32[3,384,96]{1,2,0:T(8,128)}, f32[96,384]{1,0:T(8,128)}, f32[384,384]{1,0:T(8,128)}, ...) | async-done | bytes 1769488 | tf_op jit(solution)/shard_map/psum | solution.py:223
  881.6 35.2 %reduce-scatter.11.cloned.1.call-done = bf16[2,576,384]{2,1,0:T(8,128)(2,1)} async-done(((bf16[2,2304,384]{2,1,0:T(8,128)(2,1)}), bf16[2,576,384]{2,1,0:T(8,128)(2,1)}) %reduce-scatter.11.cloned.1.call-update) | async-done | bytes 884752 | tf_op jit(solution)/shard_map/reduce_scatter | solution.py:200
  920.4 39.9 %all-reduce = (f32[]{:T(128)}, f32[9,384]{1,0:T(8,128)}) all-reduce(f32[]{:T(128)S(6)} %div.48, f32[9,384]{1,0:T(8,128)S(1)} %stack.61), channel_id=1, replica_groups=mesh['dp'=8,'tp'=4] {'dp','tp'}, use_global_device_ids=true, to_apply=%region_11.12 | all-reduce | flops 3457 | bytes 27656 | tf_op jit(solution)/shard_map/psum | solution.py:226
  (291 shorter events, 161.6 us)
Async XLA Ops:
  7.2 273.7 %copy-start = (bf16[2,576,384]{2,1,0:T(8,128)(2,1)S(1)}, bf16[2,576,384]{2,1,0:T(8,128)(2,1)}, u32[]{:S(2)}) copy-start(bf16[2,576,384]{2,1,0:T(8,128)(2,1)} %param.30) | copy-start | bytes 2654212
  7.2 41.8 %copy-start.38 = (f32[3,384,96]{1,2,0:T(8,128)S(1)}, f32[3,384,96]{1,2,0:T(8,128)}, u32[]{:S(2)}) copy-start(f32[3,384,96]{1,2,0:T(8,128)} %param.33) | copy-start | bytes 1327108
  7.2 41.8 %all-gather.4.cloned.1.call-start = ((), (), s32[]{:S(2)}) async-start(), calls=%async_computation.4 | async-start | bytes 4423680 | tf_op jit(solution)/shard_map/all_gather | solution.py:142
  15.4 174.5 %reduce-scatter.5.cloned.1.call-start = ((), (), s32[]{:S(2)}) async-start(), calls=%async_computation.5 | async-start | bytes 8847360 | tf_op jit(solution)/shard_map/reduce_scatter | solution.py:147
  62.9 57.2 %copy-start.20 = (f32[96,384]{1,0:T(8,128)S(1)}, f32[96,384]{1,0:T(8,128)}, u32[]{:S(2)}) copy-start(f32[96,384]{1,0:T(8,128)} %param.34) | copy-start | bytes 442372
  126.0 63.9 %copy-start.6 = (bf16[2,576,384]{2,1,0:T(8,128)(2,1)S(1)}, bf16[2,576,384]{2,1,0:T(8,128)(2,1)}, u32[]{:S(2)}) copy-start(bf16[2,576,384]{2,1,0:T(8,128)(2,1)} %param.29) | copy-start | bytes 2654212
  126.0 63.9 %copy-start.50 = (f32[384]{0:T(512)S(1)}, f32[384]{0:T(512)}, u32[]{:S(2)}) copy-start(f32[384]{0:T(512)} %get-tuple-element.155) | copy-start | bytes 4612
  126.0 63.9 %copy-start.56 = (f32[384]{0:T(512)S(1)}, f32[384]{0:T(512)}, u32[]{:S(2)}) copy-start(f32[384]{0:T(512)} %get-tuple-element.152) | copy-start | bytes 4612
  126.0 218.7 %reduce-scatter.7.cloned.1.call-start = ((), (), s32[]{:S(2)}) async-start(), calls=%async_computation.6 | async-start | bytes 8847360 | tf_op jit(solution)/shard_map/reduce_scatter | solution.py:158
  192.7 21.5 %collective-permute-start = (bf16[2,576,384]{2,1,0:T(8,128)(2,1)S(1)}, bf16[2,576,384]{2,1,0:T(8,128)(2,1)}, u32[]{:S(2)}, u32[]{:S(2)}) collective-permute-start(bf16[2,576,384]{2,1,0:T(8,128)(2,1)S(1)} %add_convert_fusion.1), channel_id=1, source_target_pairs={{0,1},{1,2},{2,3},{3,0},{4,5},{5,6},{6,7},{7,4},{8,9},{9,10},{10,1... | collective-permute-start | bytes 2654216 | tf_op jit(solution)/shard_map/ppermute | solution.py:24
  192.8 48.6 %collective-permute-start.1 = (bf16[2,576,384]{2,1,0:T(8,128)(2,1)S(1)}, bf16[2,576,384]{2,1,0:T(8,128)(2,1)}, u32[]{:S(2)}, u32[]{:S(2)}) collective-permute-start(bf16[2,576,384]{2,1,0:T(8,128)(2,1)S(1)} %add_convert_fusion.1), channel_id=1, source_target_pairs={{0,3},{1,0},{2,1},{3,2},{4,7},{5,4},{6,5},{7,6},{8,11},{9,8},{10,9... | collective-permute-start | bytes 2654216 | tf_op jit(solution)/shard_map/ppermute | solution.py:29
  214.2 41.0 %collective-permute-start.2 = (bf16[2,576,384]{2,1,0:T(8,128)(2,1)}, bf16[2,576,384]{2,1,0:T(8,128)(2,1)}, u32[]{:S(2)}, u32[]{:S(2)}) collective-permute-start(bf16[2,576,384]{2,1,0:T(8,128)(2,1)} %collective-permute-done), channel_id=1, source_target_pairs={{0,1},{1,2},{2,3},{3,0},{4,5},{5,6},{6,7},{7,4},{8,9},{9,10},{10,1... | collective-permute-start | bytes 2654216 | tf_op jit(solution)/shard_map/ppermute | solution.py:24
  280.0 64.7 %copy-start.54 = (f32[384]{0:T(512)S(1)}, f32[384]{0:T(512)}, u32[]{:S(2)}) copy-start(f32[384]{0:T(512)} %get-tuple-element.148) | copy-start | bytes 4612
  280.0 64.7 %copy-start.55 = (f32[384]{0:T(512)S(1)}, f32[384]{0:T(512)}, u32[]{:S(2)}) copy-start(f32[384]{0:T(512)} %get-tuple-element.151) | copy-start | bytes 4612
  280.1 103.1 %all-gather.6.cloned.1.call-start = ((), (), s32[]{:S(2)}) async-start(), calls=%async_computation.7 | async-start | bytes 4423680 | tf_op jit(solution)/shard_map/all_gather | solution.py:176
  282.5 64.0 %copy-start.18 = (f32[384,384]{1,0:T(8,128)S(1)}, f32[384,384]{1,0:T(8,128)}, u32[]{:S(2)}) copy-start(f32[384,384]{1,0:T(8,128)} %param.38) | copy-start | bytes 1769476
  282.5 64.1 %copy-start.71 = (f32[384]{0:T(512)S(1)}, f32[384]{0:T(512)}, u32[]{:S(2)}) copy-start(f32[384]{0:T(512)} %get-tuple-element.147) | copy-start | bytes 4612
  352.2 110.9 %reduce-scatter.9.cloned.1.call-start = ((), (), s32[]{:S(2)}) async-start(), calls=%async_computation.8 | async-start | bytes 8847360 | tf_op jit(solution)/shard_map/reduce_scatter | solution.py:182
  399.2 63.9 %copy-start.53 = (f32[384]{0:T(512)S(1)}, f32[384]{0:T(512)}, u32[]{:S(2)}) copy-start(f32[384]{0:T(512)} %get-tuple-element.150) | copy-start | bytes 4612
  399.2 66.9 %copy-start.51 = (f32[384]{0:T(512)S(1)}, f32[384]{0:T(512)}, u32[]{:S(2)}) copy-start(f32[384]{0:T(512)} %get-tuple-element.155) | copy-start | bytes 4612
  399.2 66.9 %copy-start.57 = (f32[384]{0:T(512)S(1)}, f32[384]{0:T(512)}, u32[]{:S(2)}) copy-start(f32[384]{0:T(512)} %get-tuple-element.152) | copy-start | bytes 4612
  399.2 103.3 %all-gather.8.cloned.1.call-start = ((), (), s32[]{:S(2)}) async-start(), calls=%async_computation.9 | async-start | bytes 4423680 | tf_op jit(solution)/shard_map/all_gather | solution.py:193
  471.6 315.8 %all-reduce.5.cloned.1.call-start = ((), (), s32[]{:S(2)}) async-start(), calls=%async_computation.10 | async-start | bytes 1179648 | tf_op jit(solution)/shard_map/psum | solution.py:226
  473.2 400.9 %all-reduce.7.cloned.1.call-start = ((), (), s32[]{:S(2)}) async-start(), calls=%async_computation.12 | async-start | bytes 3538944 | tf_op jit(solution)/shard_map/psum | solution.py:223
  779.0 137.8 %reduce-scatter.11.cloned.1.call-start = ((), (), s32[]{:S(2)}) async-start(), calls=%async_computation.11 | async-start | bytes 4423680 | tf_op jit(solution)/shard_map/reduce_scatter | solution.py:200
  784.0 29.1 %copy-start.62 = (f32[384]{0:T(512)S(1)}, f32[384]{0:T(512)}, u32[]{:S(2)}) copy-start(f32[384]{0:T(512)} %get-tuple-element.135) | copy-start | bytes 4612
  784.0 29.7 %copy-start.61 = (f32[384]{0:T(512)S(1)}, f32[384]{0:T(512)}, u32[]{:S(2)}) copy-start(f32[384]{0:T(512)} %get-tuple-element.142) | copy-start | bytes 4612
  784.0 90.0 %copy-start.22 = (f32[96,384]{1,0:T(8,128)S(1)}, f32[96,384]{1,0:T(8,128)}, u32[]{:S(2)}) copy-start(f32[96,384]{1,0:T(8,128)} %param.34) | copy-start | bytes 442372
  784.0 90.0 %copy-start.42 = (f32[96,384]{1,0:T(8,128)S(1)}, f32[96,384]{1,0:T(8,128)}, u32[]{:S(2)}) copy-start(f32[96,384]{1,0:T(8,128)} %param.48) | copy-start | bytes 442372
  784.0 90.0 %copy-start.43 = (f32[96,384]{1,0:T(8,128)S(1)}, f32[96,384]{1,0:T(8,128)}, u32[]{:S(2)}) copy-start(f32[96,384]{1,0:T(8,128)} %param.41) | copy-start | bytes 442372
  784.0 91.8 %copy-start.39 = (f32[3,384,96]{1,2,0:T(8,128)S(1)}, f32[3,384,96]{1,2,0:T(8,128)}, u32[]{:S(2)}) copy-start(f32[3,384,96]{1,2,0:T(8,128)} %param.33) | copy-start | bytes 1327108
  784.0 91.8 %copy-start.40 = (f32[3,384,96]{1,2,0:T(8,128)S(1)}, f32[3,384,96]{1,2,0:T(8,128)}, u32[]{:S(2)}) copy-start(f32[3,384,96]{1,2,0:T(8,128)} %param.47) | copy-start | bytes 1327108
  784.1 91.8 %copy-start.41 = (f32[3,384,96]{1,2,0:T(8,128)S(1)}, f32[3,384,96]{1,2,0:T(8,128)}, u32[]{:S(2)}) copy-start(f32[3,384,96]{1,2,0:T(8,128)} %param.40) | copy-start | bytes 1327108
  789.8 88.2 %copy-start.16 = (f32[384,384]{1,0:T(8,128)S(1)}, f32[384,384]{1,0:T(8,128)}, u32[]{:S(2)}) copy-start(f32[384,384]{1,0:T(8,128)} %param.35) | copy-start | bytes 1769476
  789.8 88.2 %copy-start.30 = (f32[384,384]{1,0:T(8,128)S(1)}, f32[384,384]{1,0:T(8,128)}, u32[]{:S(2)}) copy-start(f32[384,384]{1,0:T(8,128)} %param.49) | copy-start | bytes 1769476
  789.8 88.2 %copy-start.31 = (f32[384,384]{1,0:T(8,128)S(1)}, f32[384,384]{1,0:T(8,128)}, u32[]{:S(2)}) copy-start(f32[384,384]{1,0:T(8,128)} %param.42) | copy-start | bytes 1769476
  879.4 37.4 %copy-start.7 = (bf16[2,576,384]{2,1,0:T(8,128)(2,1)S(1)}, bf16[2,576,384]{2,1,0:T(8,128)(2,1)}, u32[]{:S(2)}) copy-start(bf16[2,576,384]{2,1,0:T(8,128)(2,1)} %param.29) | copy-start | bytes 2654212
  879.4 37.4 %copy-start.45 = (f32[2,576]{1,0:T(2,128)S(1)}, f32[2,576]{1,0:T(2,128)}, u32[]{:S(2)}) copy-start(f32[2,576]{1,0:T(2,128)} %copy-done.44) | copy-start | bytes 13828
  879.4 37.4 %copy-start.47 = (f32[2,576]{1,0:T(2,128)S(1)}, f32[2,576]{1,0:T(2,128)}, u32[]{:S(2)}) copy-start(f32[2,576]{1,0:T(2,128)} %copy-done.46) | copy-start | bytes 13828
  879.5 37.4 %copy-start.49 = (f32[384]{0:T(512)S(1)}, f32[384]{0:T(512)}, u32[]{:S(2)}) copy-start(f32[384]{0:T(512)} %copy-done.48) | copy-start | bytes 4612
  880.2 39.4 %copy-start.63 = (f32[1,384]{1,0:T(1,128)S(1)}, f32[1,384]{1,0:T(1,128)}, u32[]{:S(2)}) copy-start(f32[1,384]{1,0:T(1,128)} %stack.60) | copy-start | bytes 4612
  880.2 39.4 %copy-start.64 = (f32[1,384]{1,0:T(1,128)S(1)}, f32[1,384]{1,0:T(1,128)}, u32[]{:S(2)}) copy-start(f32[1,384]{1,0:T(1,128)} %stack.59) | copy-start | bytes 4612
  880.2 39.4 %copy-start.65 = (f32[1,384]{1,0:T(1,128)S(1)}, f32[1,384]{1,0:T(1,128)}, u32[]{:S(2)}) copy-start(f32[1,384]{1,0:T(1,128)} %stack.58) | copy-start | bytes 4612
  880.2 39.4 %copy-start.66 = (f32[1,384]{1,0:T(1,128)S(1)}, f32[1,384]{1,0:T(1,128)}, u32[]{:S(2)}) copy-start(f32[1,384]{1,0:T(1,128)} %stack.56) | copy-start | bytes 4612
  880.2 39.4 %copy-start.67 = (f32[1,384]{1,0:T(1,128)S(1)}, f32[1,384]{1,0:T(1,128)}, u32[]{:S(2)}) copy-start(f32[1,384]{1,0:T(1,128)} %stack.57) | copy-start | bytes 4612
  880.3 39.4 %copy-start.68 = (f32[1,384]{1,0:T(1,128)S(1)}, f32[1,384]{1,0:T(1,128)}, u32[]{:S(2)}) copy-start(f32[1,384]{1,0:T(1,128)} %stack.55) | copy-start | bytes 4612
  880.3 39.4 %copy-start.69 = (f32[1,384]{1,0:T(1,128)S(1)}, f32[1,384]{1,0:T(1,128)}, u32[]{:S(2)}) copy-start(f32[1,384]{1,0:T(1,128)} %stack.54) | copy-start | bytes 4612
  880.3 81.5 %copy-start.9 = (f32[2,576,384]{2,1,0:T(8,128)S(1)}, f32[2,576,384]{2,1,0:T(8,128)}, u32[]{:S(2)}) copy-start(f32[2,576,384]{2,1,0:T(8,128)} %copy-done.8) | copy-start | bytes 5308420
  (46 other events, 224.1 us)
Sparse Core Ops, SparseCore 0:
  15.5 33.4 all-gather.3
  126.2 63.7 reduce-scatter.4
  280.2 64.4 reduce-scatter.6
  352.3 30.7 all-gather.5
  399.3 63.6 reduce-scatter.8
  471.7 30.8 all-gather.7
  509.2 127.2 all-reduce.4
  779.1 94.8 all-reduce.6
  876.8 40.0 reduce-scatter.10
